TPU v7x, 32 devices: a whole 2x2x4 slice. The times are simulated.
32 devices in a mesh: row: 16 (over z, y, x), col: 2 (over core).
Axes of the slice: x: 2, y: 2, z: 4, core: 2. Of those that a mesh axis runs over, the one named last changes fastest.
Arguments:
- matrix: float32 [4096, 4096], P('row', 'col'), may hold values from -15.625 to 15.625
Outputs:
- r_top: float32 [512, 4096], P(None, 'col')
- basis: float32 [4096, 512], P('row')
All inputs are finite; a program needn't handle non-finite values.
Results may differ from a plain program's by a relative error of at most 0.0003.
Values sent between devices are 32-bit elements; how exact they have to be, the bound alone decides.
A program may use at most 64 MiB of HBM per device.

v0:
```python
import math
import jax
import jax.numpy as jnp
from jax import lax
from jax.sharding import PartitionSpec as P

PANEL = 256


def spread(value, axis, source):
    kept = jnp.where(lax.axis_index(axis) == source, value, 0).astype(value.dtype)
    return lax.psum(kept, axis)


def inner(left, right):
    return lax.dot_general(
        left,
        right,
        (((0,), (0,)), ((), ())),
        precision=lax.Precision.HIGHEST,
        preferred_element_type=jnp.float32,
    )


def product(left, right):
    return jnp.dot(left, right, precision=lax.Precision.HIGHEST, preferred_element_type=jnp.float32)


def factor(gram, valid):
    width = gram.shape[0]
    identity = jnp.eye(width, dtype=jnp.float32)
    safe_gram = jnp.where(valid, gram, identity)
    lower_factor = jnp.linalg.cholesky(safe_gram)
    lower_inverse = lax.linalg.triangular_solve(lower_factor, identity, left_side=True, lower=True)
    return (lower_factor.T, lower_inverse.T)


def body(matrix):
    panel_cols = PANEL
    rows_all = matrix.shape[0] * lax.axis_size("row")
    holder = lax.axis_index("col") == 0
    panels = matrix[:, : 2 * panel_cols]
    first_panel = panels[:, :panel_cols]
    second_panel = panels[:, panel_cols:]
    first_gram = lax.psum(inner(first_panel, first_panel), "row")
    upper_first, inverse_first = factor(first_gram, holder)
    basis_first = product(first_panel, inverse_first)
    basis_first = spread(basis_first, "col", 0)
    local_terms = inner(basis_first, matrix)
    summed, panel_gram = lax.psum((local_terms, inner(second_panel, second_panel)), "row")
    coupling = summed[:, panel_cols : 2 * panel_cols]
    remainder = matrix - product(basis_first, summed)
    second_updated = remainder[:, panel_cols : 2 * panel_cols]
    second_gram = panel_gram - inner(coupling, coupling)
    upper_second, inverse_second = factor(second_gram, holder)
    basis_second = product(second_updated, inverse_second)
    basis_second = spread(basis_second, "col", 0)
    second_proj = lax.psum(inner(basis_second, remainder), "row")
    zeros = jnp.zeros((panel_cols, panel_cols), jnp.float32)
    first_rows = jnp.where(
        holder, jnp.concatenate([upper_first, summed[:, panel_cols:]], axis=1), summed
    )
    second_rows = jnp.where(
        holder,
        jnp.concatenate([zeros, upper_second, second_proj[:, 2 * panel_cols :]], axis=1),
        second_proj,
    )
    top = jnp.concatenate([first_rows, second_rows], axis=0)
    basis = jnp.concatenate([basis_first, basis_second], axis=1) * math.sqrt(rows_all)
    return (top, basis)


def solution(mesh):
    return jax.shard_map(
        body,
        mesh=mesh,
        in_specs=(P("row", "col"),),
        out_specs=(P(None, "col"), P("row", None)),
        check_vma=False,
    )
```

profile of v0, /device:TPU:1, one launch (start us, length us, event | category | flops | bytes accessed | tf_op | source)
XLA Modules:
  0.0 589.3 jit_solution(6052217583035175400)
XLA Ops:
  7.2 2.3 fusion.18
  9.7 111.9 %all-reduce.8.cloned.1.call-done = f32[256,256]{0,1:T(8,128)} async-done(((f32[256,256]{0,1:T(8,128)}), f32[256,256]{0,1:T(8,128)}) %all-reduce.8.cloned.1.call-update) | async-done | bytes 262160 | tf_op jit(solution)/shard_map/psum | solution.py:45
  121.8 11.7 %cholesky.130 = f32[128,128]{1,0:T(8,128)S(1)} custom-call(f32[128,128]{1,0:T(8,128)S(1)} %cholesky.194), custom_call_target="Cholesky" | custom-call | tf_op jit(solution)/shard_map/jit(cholesky)/cholesky | solution.py:33
  133.6 9.8 %custom-call.13 = f32[1,128,128]{1,2,0:T(8,128)S(1)} custom-call(f32[1,128,128]{2,1,0:T(8,128)S(1)} %get-tuple-element.55), custom_call_target="InvertDiagBlocksLowerTriangular" | custom-call | tf_op jit(solution)/shard_map/jit(cholesky)/cholesky | solution.py:33
  143.9 11.7 %cholesky.147 = f32[128,128]{1,0:T(8,128)S(1)} custom-call(f32[128,128]{1,0:T(8,128)S(1)} %convolution_subtract_fusion.5), custom_call_target="Cholesky" | custom-call | tf_op jit(solution)/shard_map/jit(cholesky)/cholesky | solution.py:33
  157.6 15.5 %while.4 = (s32[]{:T(128)}, f32[256,256]{1,0:T(8,128)S(1)}, s32[2,2]{1,0:T(2,128)S(1)}, f32[2,128,128]{2,1,0:T(8,128)S(1)}, s32[]{:T(128)}) while((s32[]{:T(128)}, f32[256,256]{1,0:T(8,128)S(1)}, s32[2,2]{1,0:T(2,128)S(1)}, f32[2,128,128]{2,1,0:T(8,128)S(1)}, s32[]{:T(128)}) %tuple.50), condition=%wide.while_cond, body=%wide.while_body.sunk | while | flops 2 | bytes 131189 | solution.py:34
  170.0 1.3 bitcast_dynamic-update-slice_fusion.4
  171.9 1.3 bitcast_dynamic-update-slice_fusion.4
  173.2 19.7 %custom-call.14 = f32[2,128,128]{1,2,0:T(8,128)S(1)} custom-call(f32[2,128,128]{2,1,0:T(8,128)S(1)} %get-tuple-element.18), custom_call_target="InvertDiagBlocksLowerTriangular" | custom-call | tf_op jit(solution)/shard_map/triangular_solve/custom-call.0 | solution.py:34
  193.9 1.1 fusion.1
  195.1 1.3 fusion.14
  196.4 20.3 %all-reduce.10.cloned.1.call-done = f32[256,256]{0,1:T(8,128)} async-done(((f32[256,256]{0,1:T(8,128)}), f32[256,256]{0,1:T(8,128)}) %all-reduce.10.cloned.1.call-update) | async-done | bytes 262160 | tf_op jit(solution)/shard_map/psum | solution.py:12
  216.8 4.2 fusion.41
  221.0 134.4 %all-reduce.16.cloned.1.call-done = (f32[256,2048]{1,0:T(8,128)}, f32[256,256]{0,1:T(8,128)}) async-done(((f32[256,2048]{1,0:T(8,128)}, f32[256,256]{0,1:T(8,128)}), (f32[256,2048]{1,0:T(8,128)}, f32[256,256]{0,1:T(8,128)})) %all-reduce.16.cloned.1.call-update) | async-done | bytes 2359312 | tf_op jit(solution)/shard_map/psum | solution.py:50
  355.4 1.7 fusion
  357.3 11.7 %cholesky.164 = f32[128,128]{1,0:T(8,128)S(1)} custom-call(f32[128,128]{1,0:T(8,128)S(1)} %cholesky.197), custom_call_target="Cholesky" | custom-call | tf_op jit(solution)/shard_map/jit(cholesky)/cholesky | solution.py:33
  369.7 9.8 %custom-call.15 = f32[1,128,128]{1,2,0:T(8,128)S(1)} custom-call(f32[1,128,128]{2,1,0:T(8,128)S(1)} %get-tuple-element.51), custom_call_target="InvertDiagBlocksLowerTriangular" | custom-call | tf_op jit(solution)/shard_map/jit(cholesky)/cholesky | solution.py:33
  380.0 11.7 %cholesky.181 = f32[128,128]{1,0:T(8,128)S(1)} custom-call(f32[128,128]{1,0:T(8,128)S(1)} %convolution_subtract_fusion.4), custom_call_target="Cholesky" | custom-call | tf_op jit(solution)/shard_map/jit(cholesky)/cholesky | solution.py:33
  394.5 4.1 while.5
  395.3 1.4 bitcast_dynamic-update-slice_fusion.5
  397.3 1.4 bitcast_dynamic-update-slice_fusion.5
  398.6 19.7 %custom-call.16 = f32[2,128,128]{1,2,0:T(8,128)S(1)} custom-call(f32[2,128,128]{2,1,0:T(8,128)S(1)} %get-tuple-element.19), custom_call_target="InvertDiagBlocksLowerTriangular" | custom-call | tf_op jit(solution)/shard_map/triangular_solve/custom-call.0 | solution.py:34
  419.4 3.5 convolution_subtract_fusion
  422.9 1.3 copy-done.2
  425.4 18.0 %all-reduce.12.cloned.1.call-done = f32[256,256]{0,1:T(8,128)} async-done(((f32[256,256]{0,1:T(8,128)}), f32[256,256]{0,1:T(8,128)}) %all-reduce.12.cloned.1.call-update) | async-done | bytes 262160 | tf_op jit(solution)/shard_map/psum | solution.py:12
  443.4 4.9 fusion.42
  448.4 1.4 slice.98
  450.0 3.1 maximum_select_fusion
  454.1 122.1 %all-reduce.14.cloned.1.call-done = f32[256,2048]{1,0:T(8,128)} async-done(((f32[256,2048]{1,0:T(8,128)}), f32[256,2048]{1,0:T(8,128)}) %all-reduce.14.cloned.1.call-update) | async-done | bytes 2097168 | tf_op jit(solution)/shard_map/psum | solution.py:58
  576.3 1.4 slice-done
  577.7 2.0 maximum_select_fusion.1
  579.9 2.5 pad_maximum_fusion
  (71 shorter events, 11.6 us)
Async XLA Ops:
  7.2 114.4 %all-reduce.8.cloned.1.call-start = ((), (), s32[]{:S(2)}) async-start(), calls=%async_computation | async-start | bytes 524288 | tf_op jit(solution)/shard_map/psum | solution.py:45
  9.6 207.2 %all-reduce.10.cloned.1.call-start = ((), (), s32[]{:S(2)}) async-start(), calls=%async_computation.1 | async-start | bytes 524288 | tf_op jit(solution)/shard_map/psum | solution.py:12
  121.8 72.1 %copy-start.1 = (f32[256,2048]{1,0:T(8,128)S(1)}, f32[256,2048]{1,0:T(8,128)}, u32[]{:S(2)}) copy-start(f32[256,2048]{1,0:T(8,128)} %param.4) | copy-start | bytes 6291460
  195.1 160.3 %all-reduce.16.cloned.1.call-start = ((), (), s32[]{:S(2)}) async-start(), calls=%async_computation.4 | async-start | bytes 4718592 | tf_op jit(solution)/shard_map/psum | solution.py:50
  221.0 222.4 %all-reduce.12.cloned.1.call-start = ((), (), s32[]{:S(2)}) async-start(), calls=%async_computation.2 | async-start | bytes 524288 | tf_op jit(solution)/shard_map/psum | solution.py:12
  357.3 62.1 %copy-start = (f32[256,2048]{1,0:T(8,128)S(1)}, f32[256,2048]{1,0:T(8,128)}, u32[]{:S(2)}) copy-start(f32[256,2048]{1,0:T(8,128)} %get-tuple-element.38) | copy-start | bytes 6291460
  357.3 62.1 %copy-start.4 = (f32[256,256]{0,1:T(8,128)S(1)}, f32[256,256]{0,1:T(8,128)}, u32[]{:S(2)}) copy-start(f32[256,256]{0,1:T(8,128)} %all-reduce.10.cloned.1.call-done) | copy-start | bytes 786436
  422.9 1.3 copy-start.2
  425.4 150.9 %all-reduce.14.cloned.1.call-start = ((), (), s32[]{:S(2)}) async-start(), calls=%async_computation.3 | async-start | bytes 4194304 | tf_op jit(solution)/shard_map/psum | solution.py:58
  448.3 1.5 copy-start.6
  450.0 3.1 copy-start.5
  576.3 1.4 slice-start
  577.7 2.2 copy-start.3
Sparse Core Ops, SparseCore 0:
  13.8 107.7 all-reduce.7
  195.2 21.5 all-reduce.9
  222.9 132.4 all-reduce.15
  425.5 17.8 all-reduce.11
  448.7 127.5 all-reduce.13
where the time goes:
time: 598 us; the launch traced here: 589 us
  waiting for transfers between devices  407 us (68%)
  other arithmetic  117 us (20%)
  matrix products  23.2 us (4%)
  between operations  17 us (3%)
  local copies, waits for them, and re-layouts  13.6 us (2%)
  loops' own time  12 us (2%)
    psum x1, waiting for transfers between devices, body(): lax.psum((local_terms, inner(second_panel, second_panel)), 'row')  134 us
    psum x1, waiting for transfers between devices, body(): second_proj = lax.psum(inner(basis_second, remainder), 'row')  122 us
    psum x1, waiting for transfers between devices, body(): first_gram = lax.psum(inner(first_panel, first_panel), 'row')  112 us
    another operation x13, other arithmetic, factor(): lower_factor = jnp.linalg.cholesky(safe_gram)  68.5 us
    another operation x3, other arithmetic, factor(): lax.linalg.triangular_solve(lower_factor, identity, left_side=True, lower...  39.4 us
    psum x2, waiting for transfers between devices, spread(): return lax.psum(kept, axis)  38.3 us
    dot_general x5, matrix products, inner(): lax.dot_general(left, right, (((0,), (0,)), ((), ())), precision=lax.Prec...  14.4 us
    another operation x2, loops' own time, factor(): lax.linalg.triangular_solve(lower_factor, identity, left_side=True, lower...  12 us
  transfers between devices with their start and end apart: 5, of which 5 were waited for; matrix products, arithmetic and copies ran while one was open for 1% of the time, Pallas kernels for 0%

commit v1 on v0

--- a/solution.py
+++ b/solution.py
@@ -42,7 +42,7 @@
     panels = matrix[:, : 2 * panel_cols]
     first_panel = panels[:, :panel_cols]
     second_panel = panels[:, panel_cols:]
-    first_gram = lax.psum(inner(first_panel, first_panel), "row")
+    first_gram = jnp.sum(jax.lax.all_gather(inner(first_panel, first_panel), "row"), axis=0)
     upper_first, inverse_first = factor(first_gram, holder)
     basis_first = product(first_panel, inverse_first)
     basis_first = spread(basis_first, "col", 0)

time: 598 us -> 564 us (0.943)
  waiting for transfers between devices: 407 us -> 370 us
    psum x1 -> x0, waiting for transfers between devices: 112 us -> none  [body(): first_gram = lax.psum(inner(first_panel, first_panel), 'row')]
    all_gather x0 -> x1, waiting for transfers between devices: none -> 77.7 us  [body(): jax.lax.all_gather(inner(first_panel, first_panel), 'row')]
where the time goes in v1:
time: 564 us; the launch traced here: 555 us
  waiting for transfers between devices  370 us (66%)
  other arithmetic  119 us (21%)
  matrix products  23.2 us (4%)
  between operations  17 us (3%)
  local copies, waits for them, and re-layouts  13.8 us (2%)
  loops' own time  12 us (2%)
    psum x1, waiting for transfers between devices, body(): lax.psum((local_terms, inner(second_panel, second_panel)), 'row')  134 us
    psum x1, waiting for transfers between devices, body(): second_proj = lax.psum(inner(basis_second, remainder), 'row')  122 us
    all_gather x1, waiting for transfers between devices, body(): jax.lax.all_gather(inner(first_panel, first_panel), 'row')  77.7 us
    another operation x13, other arithmetic, factor(): lower_factor = jnp.linalg.cholesky(safe_gram)  68.5 us
    another operation x3, other arithmetic, factor(): lax.linalg.triangular_solve(lower_factor, identity, left_side=True, lower...  39.4 us
    psum x2, waiting for transfers between devices, spread(): return lax.psum(kept, axis)  35.6 us
    dot_general x5, matrix products, inner(): lax.dot_general(left, right, (((0,), (0,)), ((), ())), precision=lax.Prec...  14.4 us
    another operation x2, loops' own time, factor(): lax.linalg.triangular_solve(lower_factor, identity, left_side=True, lower...  12 us
  transfers between devices with their start and end apart: 5, of which 5 were waited for; matrix products, arithmetic and copies ran while one was open for 1% of the time, Pallas kernels for 0%

profile of v1, /device:TPU:1, one launch (start us, length us, event | category | flops | bytes accessed | tf_op | source)
XLA Modules:
  0.0 555.1 jit_solution(935020550156337219)
XLA Ops:
  7.2 2.3 fusion.18
  9.7 77.7 %all-gather.3.cloned.1.call-done = f32[4096,256]{1,0:T(8,128)} async-done(((f32[256,256]{1,0:T(8,128)}), f32[4096,256]{1,0:T(8,128)}) %all-gather.3.cloned.1.call-update) | async-done | bytes 4194320 | tf_op jit(solution)/shard_map/all_gather | solution.py:45
  87.4 2.5 reduce_sum.9
  90.2 11.7 %cholesky.130 = f32[128,128]{1,0:T(8,128)S(1)} custom-call(f32[128,128]{1,0:T(8,128)S(1)} %cholesky.194), custom_call_target="Cholesky" | custom-call | tf_op jit(solution)/shard_map/jit(cholesky)/cholesky | solution.py:33
  102.0 9.8 %custom-call.13 = f32[1,128,128]{1,2,0:T(8,128)S(1)} custom-call(f32[1,128,128]{2,1,0:T(8,128)S(1)} %get-tuple-element.57), custom_call_target="InvertDiagBlocksLowerTriangular" | custom-call | tf_op jit(solution)/shard_map/jit(cholesky)/cholesky | solution.py:33
  112.3 11.7 %cholesky.147 = f32[128,128]{1,0:T(8,128)S(1)} custom-call(f32[128,128]{1,0:T(8,128)S(1)} %convolution_subtract_fusion.5), custom_call_target="Cholesky" | custom-call | tf_op jit(solution)/shard_map/jit(cholesky)/cholesky | solution.py:33
  126.0 15.5 %while.4 = (s32[]{:T(128)}, f32[256,256]{1,0:T(8,128)S(1)}, s32[2,2]{1,0:T(2,128)S(1)}, f32[2,128,128]{2,1,0:T(8,128)S(1)}, s32[]{:T(128)}) while((s32[]{:T(128)}, f32[256,256]{1,0:T(8,128)S(1)}, s32[2,2]{1,0:T(2,128)S(1)}, f32[2,128,128]{2,1,0:T(8,128)S(1)}, s32[]{:T(128)}) %tuple.51), condition=%wide.while_cond, body=%wide.while_body.sunk | while | flops 2 | bytes 131189 | solution.py:34
  138.4 1.3 bitcast_dynamic-update-slice_fusion.4
  140.3 1.3 bitcast_dynamic-update-slice_fusion.4
  141.6 19.7 %custom-call.14 = f32[2,128,128]{1,2,0:T(8,128)S(1)} custom-call(f32[2,128,128]{2,1,0:T(8,128)S(1)} %get-tuple-element.18), custom_call_target="InvertDiagBlocksLowerTriangular" | custom-call | tf_op jit(solution)/shard_map/triangular_solve/custom-call.0 | solution.py:34
  163.5 1.3 fusion.14
  164.8 17.7 %all-reduce.7.cloned.1.call-done = f32[256,256]{0,1:T(8,128)} async-done(((f32[256,256]{0,1:T(8,128)}), f32[256,256]{0,1:T(8,128)}) %all-reduce.7.cloned.1.call-update) | async-done | bytes 262160 | tf_op jit(solution)/shard_map/psum | solution.py:12
  182.5 4.2 fusion.41
  186.7 134.4 %all-reduce.13.cloned.1.call-done = (f32[256,2048]{1,0:T(8,128)}, f32[256,256]{0,1:T(8,128)}) async-done(((f32[256,2048]{1,0:T(8,128)}, f32[256,256]{0,1:T(8,128)}), (f32[256,2048]{1,0:T(8,128)}, f32[256,256]{0,1:T(8,128)})) %all-reduce.13.cloned.1.call-update) | async-done | bytes 2359312 | tf_op jit(solution)/shard_map/psum | solution.py:50
  321.1 1.7 fusion
  323.1 11.7 %cholesky.164 = f32[128,128]{1,0:T(8,128)S(1)} custom-call(f32[128,128]{1,0:T(8,128)S(1)} %cholesky.197), custom_call_target="Cholesky" | custom-call | tf_op jit(solution)/shard_map/jit(cholesky)/cholesky | solution.py:33
  335.5 9.8 %custom-call.15 = f32[1,128,128]{1,2,0:T(8,128)S(1)} custom-call(f32[1,128,128]{2,1,0:T(8,128)S(1)} %get-tuple-element.53), custom_call_target="InvertDiagBlocksLowerTriangular" | custom-call | tf_op jit(solution)/shard_map/jit(cholesky)/cholesky | solution.py:33
  345.8 11.7 %cholesky.181 = f32[128,128]{1,0:T(8,128)S(1)} custom-call(f32[128,128]{1,0:T(8,128)S(1)} %convolution_subtract_fusion.4), custom_call_target="Cholesky" | custom-call | tf_op jit(solution)/shard_map/jit(cholesky)/cholesky | solution.py:33
  360.2 4.1 while.5
  361.0 1.4 bitcast_dynamic-update-slice_fusion.5
  363.0 1.4 bitcast_dynamic-update-slice_fusion.5
  364.4 19.7 %custom-call.16 = f32[2,128,128]{1,2,0:T(8,128)S(1)} custom-call(f32[2,128,128]{2,1,0:T(8,128)S(1)} %get-tuple-element.19), custom_call_target="InvertDiagBlocksLowerTriangular" | custom-call | tf_op jit(solution)/shard_map/triangular_solve/custom-call.0 | solution.py:34
  385.1 3.5 convolution_subtract_fusion
  388.7 1.3 copy-done.2
  391.2 18.0 %all-reduce.9.cloned.1.call-done = f32[256,256]{0,1:T(8,128)} async-done(((f32[256,256]{0,1:T(8,128)}), f32[256,256]{0,1:T(8,128)}) %all-reduce.9.cloned.1.call-update) | async-done | bytes 262160 | tf_op jit(solution)/shard_map/psum | solution.py:12
  409.2 4.9 fusion.42
  414.2 1.4 slice.98
  415.7 3.1 maximum_select_fusion
  419.9 122.1 %all-reduce.11.cloned.1.call-done = f32[256,2048]{1,0:T(8,128)} async-done(((f32[256,2048]{1,0:T(8,128)}), f32[256,2048]{1,0:T(8,128)}) %all-reduce.11.cloned.1.call-update) | async-done | bytes 2097168 | tf_op jit(solution)/shard_map/psum | solution.py:58
  542.0 1.4 slice-done
  543.4 2.0 maximum_select_fusion.1
  545.6 2.5 pad_maximum_fusion
  (73 shorter events, 12.9 us)
Async XLA Ops:
  7.2 80.2 %all-gather.3.cloned.1.call-start = ((), (), s32[]{:S(2)}) async-start(), calls=%async_computation.3 | async-start | bytes 4456448 | tf_op jit(solution)/shard_map/all_gather | solution.py:45
  9.6 172.9 %all-reduce.7.cloned.1.call-start = ((), (), s32[]{:S(2)}) async-start(), calls=%async_computation | async-start | bytes 524288 | tf_op jit(solution)/shard_map/psum | solution.py:12
  90.2 72.1 %copy-start.1 = (f32[256,2048]{1,0:T(8,128)S(1)}, f32[256,2048]{1,0:T(8,128)}, u32[]{:S(2)}) copy-start(f32[256,2048]{1,0:T(8,128)} %param.4) | copy-start | bytes 6291460
  163.5 157.7 %all-reduce.13.cloned.1.call-start = ((), (), s32[]{:S(2)}) async-start(), calls=%async_computation.4 | async-start | bytes 4718592 | tf_op jit(solution)/shard_map/psum | solution.py:50
  186.7 222.5 %all-reduce.9.cloned.1.call-start = ((), (), s32[]{:S(2)}) async-start(), calls=%async_computation.1 | async-start | bytes 524288 | tf_op jit(solution)/shard_map/psum | solution.py:12
  323.0 62.1 %copy-start = (f32[256,2048]{1,0:T(8,128)S(1)}, f32[256,2048]{1,0:T(8,128)}, u32[]{:S(2)}) copy-start(f32[256,2048]{1,0:T(8,128)} %get-tuple-element.40) | copy-start | bytes 6291460
  323.1 62.1 %copy-start.4 = (f32[256,256]{0,1:T(8,128)S(1)}, f32[256,256]{0,1:T(8,128)}, u32[]{:S(2)}) copy-start(f32[256,256]{0,1:T(8,128)} %all-reduce.7.cloned.1.call-done) | copy-start | bytes 786436
  388.7 1.3 copy-start.2
  391.1 150.9 %all-reduce.11.cloned.1.call-start = ((), (), s32[]{:S(2)}) async-start(), calls=%async_computation.2 | async-start | bytes 4194304 | tf_op jit(solution)/shard_map/psum | solution.py:58
  414.1 1.5 copy-start.6
  415.7 3.1 copy-start.5
  542.0 1.4 slice-start
  543.4 2.2 copy-start.3
Sparse Core Ops, SparseCore 0:
  11.3 76.0 all-gather.2
  163.6 18.8 all-reduce.6
  188.6 132.4 all-reduce.12
  391.2 17.8 all-reduce.8
  414.5 127.4 all-reduce.10
